TPU v7x, 256 devices: a whole 4x4x8 slice. The times are simulated.
256 devices in a mesh: row: 32 (over z, y_hi, core), off: 8 (over x, y_lo).
Axes of the slice: x: 4, y: 4 (y_hi: 2, y_lo: 2; y = y_hi * 2 + y_lo), z: 8, core: 2. Of those that a mesh axis runs over, the one named last changes fastest.
Arguments:
- vectors: float32 [32768, 128], P(('row', 'off')), may hold values from -6 to 6
- blocks: float32 [32, 8, 48, 128, 128], P('row', 'off'), may hold values from -0.0546875 to 0.0546875
- lists: int32 [32, 8, 2, 48], P('row', 'off'), may hold values from 0 to 7, as said below
Outputs:
- filtered: float32 [32768, 128], P(('row', 'off'))
Inputs may be any that keep to these rules, and one draw needn't show every extreme that they name: `lists`: within each tile the 48 listed blocks are distinct positions of its 8 x 8 grid of blocks.
All inputs are finite; a program needn't handle non-finite values.
Results may differ from a plain program's by a relative error of at most 0.00011.
Values sent between devices are 32-bit elements; how exact they have to be, the bound alone decides.
A program may use at most 64 MiB of HBM per device.

v0:
```python
import jax
import jax.numpy as jnp
from jax import lax
from jax.sharding import PartitionSpec as P

DEGREE = 4


first_scale = 0.4
later_scale = 0.8


def passed_along(block, axis, distance):
    devices = range(lax.axis_size(axis))
    route = [((i - distance) % len(devices), i) for i in devices]
    return lax.ppermute(block, axis, route)


def per_device(vectors, blocks, lists):
    n_offsets = lax.axis_size("off")
    offset_index = lax.axis_index("off")
    piece_rows = vectors.shape[0]
    tile_rows = piece_rows * n_offsets
    width = vectors.shape[1]
    block_size = blocks.shape[-1]
    per_side = tile_rows // block_size
    stored = blocks[0, 0]
    row_list = lists[0, 0, 0]
    col_list = lists[0, 0, 1]
    positions = jnp.arange(per_side, dtype=jnp.int32)
    row_onehot = (row_list[:, None] == positions[None, :]).astype(jnp.float32)
    col_onehot = (col_list[:, None] == positions[None, :]).astype(jnp.float32)
    bit_count = (n_offsets - 1).bit_length()

    def pull(field):
        for bit_number in range(bit_count):
            moved = passed_along(field, "row", -(1 << bit_number))
            field = jnp.where(offset_index // (1 << bit_number) % 2 == 1, moved, field)
        return field

    def push(field):
        for bit_number in range(bit_count):
            moved = passed_along(field, "row", 1 << bit_number)
            field = jnp.where(offset_index // (1 << bit_number) % 2 == 1, moved, field)
        return field

    def apply_tiles(gathered):
        own = gathered.reshape(per_side, block_size, width)
        transposed = jnp.einsum(
            "kab,kav->kbv", stored, own[row_list], precision=lax.Precision.HIGHEST
        )
        back_terms = jnp.einsum(
            "kt,kbv->tbv", col_onehot, transposed, precision=lax.Precision.HIGHEST
        )
        returned = push(back_terms.reshape(tile_rows, width))
        far_field = pull(gathered).reshape(per_side, block_size, width)
        direct = jnp.einsum(
            "kab,kbv->kav", stored, far_field[col_list], precision=lax.Precision.HIGHEST
        )
        ahead = jnp.einsum("kt,kav->tav", row_onehot, direct, precision=lax.Precision.HIGHEST)
        return ahead.reshape(tile_rows, width) + returned

    def spread(piece):
        return lax.all_gather(piece, "off", axis=0, tiled=True)

    def fold(terms):
        return lax.psum_scatter(terms, "off", scatter_dimension=0, tiled=True)

    previous = vectors
    current = first_scale * fold(apply_tiles(spread(vectors)))
    for degree in range(1, DEGREE):
        following = later_scale * fold(apply_tiles(spread(current))) - previous
        previous, current = (current, following)
    return current


def solution(mesh):
    in_specs = (
        P(("row", "off"), None),
        P("row", "off", None, None, None),
        P("row", "off", None, None),
    )
    out_specs = P(("row", "off"), None)
    return jax.shard_map(
        per_device, mesh=mesh, in_specs=in_specs, out_specs=out_specs, check_vma=False
    )
```

profile of v0, /device:TPU:32, one launch (start us, length us, event | category | flops | bytes accessed | tf_op | source)
XLA Modules:
  0.0 610.8 jit_solution(9065694514423480050)
XLA Ops:
  6.5 31.6 %all_gather.12 = f32[1024,128]{1,0:T(8,128)} all-gather(f32[128,128]{1,0:T(8,128)} %param.3), channel_id=1, replica_groups=mesh['row'=32,'off'=8] {'off'}, dimensions={0}, use_global_device_ids=true | all-gather | bytes 589824 | tf_op jit(solution)/shard_map/all_gather | solution.py:64
  42.4 7.9 %fusion.28 = f32[48,128,128]{2,1,0:T(8,128)} fusion(f32[48,128,128]{2,1,0:T(8,128)} %gather_fusion.1, f32[1,1,48,128,128]{4,3,2,1,0:T(8,128)S(1)} %copy-done), kind=kOutput, calls=%fused_computation.36 | convolution fusion | flops 1207959552 | bytes 9437184 | tf_op jit(solution)/shard_map/kab,kav->kbv/dot_general | solution.py:49
  50.2 3.6 copy.13
  62.9 6.2 %collective-permute-done.3 = f32[1024,128]{1,0:T(8,128)} collective-permute-done((f32[1024,128]{1,0:T(8,128)}, f32[1024,128]{1,0:T(8,128)}, u32[]{:S(2)}, u32[]{:S(2)}) %collective-permute-start.3) | collective-permute-done | bytes 524320 | tf_op jit(solution)/shard_map/ppermute | solution.py:16
  71.1 13.5 %collective-permute-start.4 = (f32[1024,128]{1,0:T(8,128)}, f32[1024,128]{1,0:T(8,128)}, u32[]{:S(2)}, u32[]{:S(2)}) collective-permute-start(f32[1024,128]{1,0:T(8,128)} %broadcast_select_fusion.6), channel_id=1, source_target_pairs={{240,0},{248,8},{0,16},{8,24},{16,32},{24,40},{32,48},{40,56},{48,... | collective-permute-start | bytes 1572872 | tf_op jit(solution)/shard_map/ppermute | solution.py:16
  86.6 10.5 %collective-permute-done.4 = f32[1024,128]{1,0:T(8,128)} collective-permute-done((f32[1024,128]{1,0:T(8,128)}, f32[1024,128]{1,0:T(8,128)}, u32[]{:S(2)}, u32[]{:S(2)}) %collective-permute-start.4) | collective-permute-done | bytes 524320 | tf_op jit(solution)/shard_map/ppermute | solution.py:16
  106.5 7.9 %fusion.30 = f32[48,128,128]{2,1,0:T(8,128)} fusion(f32[48,128,128]{2,1,0:T(8,128)} %gather_fusion, f32[1,1,48,128,128]{4,3,2,1,0:T(8,128)S(1)} %copy-done), kind=kOutput, calls=%fused_computation.38 | convolution fusion | flops 1207959552 | bytes 9437184 | tf_op jit(solution)/shard_map/kab,kbv->kav/dot_general | solution.py:57
  114.4 3.6 copy.12
  123.2 40.0 %reduce-scatter.5.cloned.1.call-done = f32[128,128]{1,0:T(8,128)} async-done(((f32[1024,128]{1,0:T(8,128)}), f32[128,128]{1,0:T(8,128)}) %reduce-scatter.5.cloned.1.call-update) | async-done | bytes 65552 | tf_op jit(solution)/shard_map/reduce_scatter | solution.py:67
  164.0 31.1 %all_gather.13 = f32[1024,128]{1,0:T(8,128)} all-gather(f32[128,128]{1,0:T(8,128)S(1)} %broadcast_multiply_fusion), channel_id=1, replica_groups=mesh['row'=32,'off'=8] {'off'}, dimensions={0}, use_global_device_ids=true | all-gather | bytes 589824 | tf_op jit(solution)/shard_map/all_gather | solution.py:64
  198.6 7.9 %fusion.24 = f32[48,128,128]{2,1,0:T(8,128)} fusion(f32[48,128,128]{2,1,0:T(8,128)} %gather_fusion.3, f32[1,1,48,128,128]{4,3,2,1,0:T(8,128)S(1)} %copy-done), kind=kOutput, calls=%fused_computation.32 | convolution fusion | flops 1207959552 | bytes 9437184 | tf_op jit(solution)/shard_map/kab,kav->kbv/dot_general | solution.py:49
  217.6 6.7 %collective-permute-done.9 = f32[1024,128]{1,0:T(8,128)S(1)} collective-permute-done((f32[1024,128]{1,0:T(8,128)S(1)}, f32[1024,128]{1,0:T(8,128)S(1)}, u32[]{:S(2)}, u32[]{:S(2)}) %collective-permute-start.9) | collective-permute-done | bytes 524320 | tf_op jit(solution)/shard_map/ppermute | solution.py:16
  224.4 12.9 %collective-permute-start.10 = (f32[1024,128]{1,0:T(8,128)S(1)}, f32[1024,128]{1,0:T(8,128)S(1)}, u32[]{:S(2)}, u32[]{:S(2)}) collective-permute-start(f32[1024,128]{1,0:T(8,128)S(1)} %broadcast_select_fusion.4), channel_id=1, source_target_pairs={{240,0},{248,8},{0,16},{8,24},{16,32},{24,40},{32,48},{40,56},{48,... | collective-permute-start | bytes 1572872 | tf_op jit(solution)/shard_map/ppermute | solution.py:16
  237.7 11.9 %collective-permute-done.10 = f32[1024,128]{1,0:T(8,128)S(1)} collective-permute-done((f32[1024,128]{1,0:T(8,128)S(1)}, f32[1024,128]{1,0:T(8,128)S(1)}, u32[]{:S(2)}, u32[]{:S(2)}) %collective-permute-start.10) | collective-permute-done | bytes 524320 | tf_op jit(solution)/shard_map/ppermute | solution.py:16
  256.4 7.9 %fusion.26 = f32[48,128,128]{2,1,0:T(8,128)} fusion(f32[48,128,128]{2,1,0:T(8,128)} %gather_fusion.2, f32[1,1,48,128,128]{4,3,2,1,0:T(8,128)S(1)} %copy-done), kind=kOutput, calls=%fused_computation.34 | convolution fusion | flops 1207959552 | bytes 9437184 | tf_op jit(solution)/shard_map/kab,kbv->kav/dot_general | solution.py:57
  273.1 36.3 %reduce-scatter.7.cloned.1.call-done = f32[128,128]{1,0:T(8,128)} async-done(((f32[1024,128]{1,0:T(8,128)}), f32[128,128]{1,0:T(8,128)}) %reduce-scatter.7.cloned.1.call-update) | async-done | bytes 65552 | tf_op jit(solution)/shard_map/reduce_scatter | solution.py:67
  310.2 31.1 %all_gather.14 = f32[1024,128]{1,0:T(8,128)} all-gather(f32[128,128]{1,0:T(8,128)S(1)} %multiply_subtract_fusion.2), channel_id=1, replica_groups=mesh['row'=32,'off'=8] {'off'}, dimensions={0}, use_global_device_ids=true | all-gather | bytes 589824 | tf_op jit(solution)/shard_map/all_gather | solution.py:64
  345.0 7.9 %fusion.20 = f32[48,128,128]{2,1,0:T(8,128)} fusion(f32[48,128,128]{2,1,0:T(8,128)} %gather_fusion.5, f32[1,1,48,128,128]{4,3,2,1,0:T(8,128)S(1)} %copy-done), kind=kOutput, calls=%fused_computation.28 | convolution fusion | flops 1207959552 | bytes 9437184 | tf_op jit(solution)/shard_map/kab,kav->kbv/dot_general | solution.py:49
  363.6 7.0 %collective-permute-done.15 = f32[1024,128]{1,0:T(8,128)S(1)} collective-permute-done((f32[1024,128]{1,0:T(8,128)S(1)}, f32[1024,128]{1,0:T(8,128)S(1)}, u32[]{:S(2)}, u32[]{:S(2)}) %collective-permute-start.15) | collective-permute-done | bytes 524320 | tf_op jit(solution)/shard_map/ppermute | solution.py:16
  370.8 12.9 %collective-permute-start.16 = (f32[1024,128]{1,0:T(8,128)S(1)}, f32[1024,128]{1,0:T(8,128)S(1)}, u32[]{:S(2)}, u32[]{:S(2)}) collective-permute-start(f32[1024,128]{1,0:T(8,128)S(1)} %broadcast_select_fusion.2), channel_id=1, source_target_pairs={{240,0},{248,8},{0,16},{8,24},{16,32},{24,40},{32,48},{40,56},{48,... | collective-permute-start | bytes 1572872 | tf_op jit(solution)/shard_map/ppermute | solution.py:16
  384.2 11.9 %collective-permute-done.16 = f32[1024,128]{1,0:T(8,128)S(1)} collective-permute-done((f32[1024,128]{1,0:T(8,128)S(1)}, f32[1024,128]{1,0:T(8,128)S(1)}, u32[]{:S(2)}, u32[]{:S(2)}) %collective-permute-start.16) | collective-permute-done | bytes 524320 | tf_op jit(solution)/shard_map/ppermute | solution.py:16
  403.2 7.9 %fusion.22 = f32[48,128,128]{2,1,0:T(8,128)} fusion(f32[48,128,128]{2,1,0:T(8,128)} %gather_fusion.4, f32[1,1,48,128,128]{4,3,2,1,0:T(8,128)S(1)} %copy-done), kind=kOutput, calls=%fused_computation.30 | convolution fusion | flops 1207959552 | bytes 9437184 | tf_op jit(solution)/shard_map/kab,kbv->kav/dot_general | solution.py:57
  419.8 36.2 %reduce-scatter.9.cloned.1.call-done = f32[128,128]{1,0:T(8,128)} async-done(((f32[1024,128]{1,0:T(8,128)}), f32[128,128]{1,0:T(8,128)}) %reduce-scatter.9.cloned.1.call-update) | async-done | bytes 65552 | tf_op jit(solution)/shard_map/reduce_scatter | solution.py:67
  456.9 31.3 %all_gather.15 = f32[1024,128]{1,0:T(8,128)} all-gather(f32[128,128]{1,0:T(8,128)S(1)} %multiply_subtract_fusion.1), channel_id=1, replica_groups=mesh['row'=32,'off'=8] {'off'}, dimensions={0}, use_global_device_ids=true | all-gather | bytes 589824 | tf_op jit(solution)/shard_map/all_gather | solution.py:64
  491.7 7.9 %fusion.16 = f32[48,128,128]{2,1,0:T(8,128)} fusion(f32[48,128,128]{2,1,0:T(8,128)} %gather_fusion.7, f32[1,1,48,128,128]{4,3,2,1,0:T(8,128)S(1)} %copy-done), kind=kOutput, calls=%fused_computation.24 | convolution fusion | flops 1207959552 | bytes 9437184 | tf_op jit(solution)/shard_map/kab,kav->kbv/dot_general | solution.py:49
  499.6 3.6 copy.19
  510.5 7.0 %collective-permute-done.21 = f32[1024,128]{1,0:T(8,128)S(1)} collective-permute-done((f32[1024,128]{1,0:T(8,128)S(1)}, f32[1024,128]{1,0:T(8,128)S(1)}, u32[]{:S(2)}, u32[]{:S(2)}) %collective-permute-start.21) | collective-permute-done | bytes 524320 | tf_op jit(solution)/shard_map/ppermute | solution.py:16
  517.5 12.6 %collective-permute-start.22 = (f32[1024,128]{1,0:T(8,128)S(1)}, f32[1024,128]{1,0:T(8,128)S(1)}, u32[]{:S(2)}, u32[]{:S(2)}) collective-permute-start(f32[1024,128]{1,0:T(8,128)S(1)} %broadcast_select_fusion), channel_id=1, source_target_pairs={{240,0},{248,8},{0,16},{8,24},{16,32},{24,40},{32,48},{40,56},{48,... | collective-permute-start | bytes 1572872 | tf_op jit(solution)/shard_map/ppermute | solution.py:16
  530.7 11.8 %collective-permute-done.22 = f32[1024,128]{1,0:T(8,128)S(1)} collective-permute-done((f32[1024,128]{1,0:T(8,128)S(1)}, f32[1024,128]{1,0:T(8,128)S(1)}, u32[]{:S(2)}, u32[]{:S(2)}) %collective-permute-start.22) | collective-permute-done | bytes 524320 | tf_op jit(solution)/shard_map/ppermute | solution.py:16
  549.2 7.9 %fusion.18 = f32[48,128,128]{2,1,0:T(8,128)} fusion(f32[48,128,128]{2,1,0:T(8,128)} %gather_fusion.6, f32[1,1,48,128,128]{4,3,2,1,0:T(8,128)S(1)} %copy-done), kind=kOutput, calls=%fused_computation.26 | convolution fusion | flops 1207959552 | bytes 9437184 | tf_op jit(solution)/shard_map/kab,kbv->kav/dot_general | solution.py:57
  557.1 3.6 copy.18
  565.9 36.5 %reduce-scatter.11.cloned.1.call-done = f32[128,128]{1,0:T(8,128)} async-done(((f32[1024,128]{1,0:T(8,128)}), f32[128,128]{1,0:T(8,128)}) %reduce-scatter.11.cloned.1.call-update) | async-done | bytes 65552 | tf_op jit(solution)/shard_map/reduce_scatter | solution.py:67
  (112 shorter events, 120.7 us)
Async XLA Ops:
  6.5 35.8 %copy-start = (f32[1,1,48,128,128]{4,3,2,1,0:T(8,128)S(1)}, f32[1,1,48,128,128]{4,3,2,1,0:T(8,128)}, u32[]{:S(2)}) copy-start(f32[1,1,48,128,128]{4,3,2,1,0:T(8,128)} %param.4) | copy-start | bytes 9437188
  6.5 156.6 %reduce-scatter.5.cloned.1.call-start = ((), (), s32[]{:S(2)}) async-start(), calls=%async_computation.4 | async-start | bytes 589824 | tf_op jit(solution)/shard_map/reduce_scatter | solution.py:67
  38.1 20.1 %collective-permute-start = (f32[1024,128]{1,0:T(8,128)}, f32[1024,128]{1,0:T(8,128)}, u32[]{:S(2)}, u32[]{:S(2)}) collective-permute-start(f32[1024,128]{1,0:T(8,128)} %all_gather.12), channel_id=1, source_target_pairs={{8,0},{16,8},{24,16},{32,24},{40,32},{48,40},{56,48},{64,56},{72,6... | collective-permute-start | bytes 1572872 | tf_op jit(solution)/shard_map/ppermute | solution.py:16
  50.2 3.6 copy-start.3
  57.7 11.4 %collective-permute-start.3 = (f32[1024,128]{1,0:T(8,128)}, f32[1024,128]{1,0:T(8,128)}, u32[]{:S(2)}, u32[]{:S(2)}) collective-permute-start(f32[1024,128]{1,0:T(8,128)} %bitcast.14), channel_id=1, source_target_pairs={{248,0},{0,8},{8,16},{16,24},{24,32},{32,40},{40,48},{48,56},{56,6... | collective-permute-start | bytes 1572872 | tf_op jit(solution)/shard_map/ppermute | solution.py:16
  60.2 24.3 %collective-permute-start.1 = (f32[1024,128]{1,0:T(8,128)}, f32[1024,128]{1,0:T(8,128)}, u32[]{:S(2)}, u32[]{:S(2)}) collective-permute-start(f32[1024,128]{1,0:T(8,128)} %broadcast_select_fusion.7), channel_id=1, source_target_pairs={{16,0},{24,8},{32,16},{40,24},{48,32},{56,40},{64,48},{72,56},{80,... | collective-permute-start | bytes 1572872 | tf_op jit(solution)/shard_map/ppermute | solution.py:16
  71.1 26.0 %collective-permute-start.4 = (f32[1024,128]{1,0:T(8,128)}, f32[1024,128]{1,0:T(8,128)}, u32[]{:S(2)}, u32[]{:S(2)}) collective-permute-start(f32[1024,128]{1,0:T(8,128)} %broadcast_select_fusion.6), channel_id=1, source_target_pairs={{240,0},{248,8},{0,16},{8,24},{16,32},{24,40},{32,48},{40,56},{48,... | collective-permute-start | bytes 1572872 | tf_op jit(solution)/shard_map/ppermute | solution.py:16
  86.4 14.7 %collective-permute-start.2 = (f32[1024,128]{1,0:T(8,128)}, f32[1024,128]{1,0:T(8,128)}, u32[]{:S(2)}, u32[]{:S(2)}) collective-permute-start(f32[1024,128]{1,0:T(8,128)} %broadcast_select_fusion.15), channel_id=1, source_target_pairs={{32,0},{40,8},{48,16},{56,24},{64,32},{72,40},{80,48},{88,56},{96,... | collective-permute-start | bytes 1572872 | tf_op jit(solution)/shard_map/ppermute | solution.py:16
  99.0 22.1 %collective-permute-start.5 = (f32[1024,128]{1,0:T(8,128)}, f32[1024,128]{1,0:T(8,128)}, u32[]{:S(2)}, u32[]{:S(2)}) collective-permute-start(f32[1024,128]{1,0:T(8,128)} %broadcast_select_fusion.14), channel_id=1, source_target_pairs={{224,0},{232,8},{240,16},{248,24},{0,32},{8,40},{16,48},{24,56},{3... | collective-permute-start | bytes 1572872 | tf_op jit(solution)/shard_map/ppermute | solution.py:16
  123.1 186.2 %reduce-scatter.7.cloned.1.call-start = ((), (), s32[]{:S(2)}) async-start(), calls=%async_computation.5 | async-start | bytes 589824 | tf_op jit(solution)/shard_map/reduce_scatter | solution.py:67
  195.1 18.6 %collective-permute-start.6 = (f32[1024,128]{1,0:T(8,128)}, f32[1024,128]{1,0:T(8,128)}, u32[]{:S(2)}, u32[]{:S(2)}) collective-permute-start(f32[1024,128]{1,0:T(8,128)} %all_gather.13), channel_id=1, source_target_pairs={{8,0},{16,8},{24,16},{32,24},{40,32},{48,40},{56,48},{64,56},{72,6... | collective-permute-start | bytes 1572872 | tf_op jit(solution)/shard_map/ppermute | solution.py:16
  213.1 11.2 %collective-permute-start.9 = (f32[1024,128]{1,0:T(8,128)S(1)}, f32[1024,128]{1,0:T(8,128)S(1)}, u32[]{:S(2)}, u32[]{:S(2)}) collective-permute-start(f32[1024,128]{1,0:T(8,128)S(1)} %bitcast.102), channel_id=1, source_target_pairs={{248,0},{0,8},{8,16},{16,24},{24,32},{32,40},{40,48},{48,56},{56,6... | collective-permute-start | bytes 1572872 | tf_op jit(solution)/shard_map/ppermute | solution.py:16
  214.8 22.5 %collective-permute-start.7 = (f32[1024,128]{1,0:T(8,128)S(1)}, f32[1024,128]{1,0:T(8,128)S(1)}, u32[]{:S(2)}, u32[]{:S(2)}) collective-permute-start(f32[1024,128]{1,0:T(8,128)S(1)} %broadcast_select_fusion.5), channel_id=1, source_target_pairs={{16,0},{24,8},{32,16},{40,24},{48,32},{56,40},{64,48},{72,56},{80,... | collective-permute-start | bytes 1572872 | tf_op jit(solution)/shard_map/ppermute | solution.py:16
  224.4 25.3 %collective-permute-start.10 = (f32[1024,128]{1,0:T(8,128)S(1)}, f32[1024,128]{1,0:T(8,128)S(1)}, u32[]{:S(2)}, u32[]{:S(2)}) collective-permute-start(f32[1024,128]{1,0:T(8,128)S(1)} %broadcast_select_fusion.4), channel_id=1, source_target_pairs={{240,0},{248,8},{0,16},{8,24},{16,32},{24,40},{32,48},{40,56},{48,... | collective-permute-start | bytes 1572872 | tf_op jit(solution)/shard_map/ppermute | solution.py:16
  237.3 14.8 %collective-permute-start.8 = (f32[1024,128]{1,0:T(8,128)S(1)}, f32[1024,128]{1,0:T(8,128)S(1)}, u32[]{:S(2)}, u32[]{:S(2)}) collective-permute-start(f32[1024,128]{1,0:T(8,128)S(1)} %broadcast_select_fusion.13), channel_id=1, source_target_pairs={{32,0},{40,8},{48,16},{56,24},{64,32},{72,40},{80,48},{88,56},{96,... | collective-permute-start | bytes 1572872 | tf_op jit(solution)/shard_map/ppermute | solution.py:16
  250.5 20.6 %collective-permute-start.11 = (f32[1024,128]{1,0:T(8,128)}, f32[1024,128]{1,0:T(8,128)}, u32[]{:S(2)}, u32[]{:S(2)}) collective-permute-start(f32[1024,128]{1,0:T(8,128)} %broadcast_select_fusion.12), channel_id=1, source_target_pairs={{224,0},{232,8},{240,16},{248,24},{0,32},{8,40},{16,48},{24,56},{3... | collective-permute-start | bytes 1572872 | tf_op jit(solution)/shard_map/ppermute | solution.py:16
  267.9 41.5 %copy-start.1 = (f32[128,128]{1,0:T(8,128)S(1)}, f32[128,128]{1,0:T(8,128)}, u32[]{:S(2)}) copy-start(f32[128,128]{1,0:T(8,128)} %param.3) | copy-start | bytes 196612
  273.0 183.0 %reduce-scatter.9.cloned.1.call-start = ((), (), s32[]{:S(2)}) async-start(), calls=%async_computation.6 | async-start | bytes 589824 | tf_op jit(solution)/shard_map/reduce_scatter | solution.py:67
  341.3 18.8 %collective-permute-start.12 = (f32[1024,128]{1,0:T(8,128)}, f32[1024,128]{1,0:T(8,128)}, u32[]{:S(2)}, u32[]{:S(2)}) collective-permute-start(f32[1024,128]{1,0:T(8,128)} %all_gather.14), channel_id=1, source_target_pairs={{8,0},{16,8},{24,16},{32,24},{40,32},{48,40},{56,48},{64,56},{72,6... | collective-permute-start | bytes 1572872 | tf_op jit(solution)/shard_map/ppermute | solution.py:16
  359.5 11.2 %collective-permute-start.15 = (f32[1024,128]{1,0:T(8,128)S(1)}, f32[1024,128]{1,0:T(8,128)S(1)}, u32[]{:S(2)}, u32[]{:S(2)}) collective-permute-start(f32[1024,128]{1,0:T(8,128)S(1)} %bitcast.103), channel_id=1, source_target_pairs={{248,0},{0,8},{8,16},{16,24},{24,32},{32,40},{40,48},{48,56},{56,6... | collective-permute-start | bytes 1572872 | tf_op jit(solution)/shard_map/ppermute | solution.py:16
  361.2 22.5 %collective-permute-start.13 = (f32[1024,128]{1,0:T(8,128)S(1)}, f32[1024,128]{1,0:T(8,128)S(1)}, u32[]{:S(2)}, u32[]{:S(2)}) collective-permute-start(f32[1024,128]{1,0:T(8,128)S(1)} %broadcast_select_fusion.3), channel_id=1, source_target_pairs={{16,0},{24,8},{32,16},{40,24},{48,32},{56,40},{64,48},{72,56},{80,... | collective-permute-start | bytes 1572872 | tf_op jit(solution)/shard_map/ppermute | solution.py:16
  370.8 25.3 %collective-permute-start.16 = (f32[1024,128]{1,0:T(8,128)S(1)}, f32[1024,128]{1,0:T(8,128)S(1)}, u32[]{:S(2)}, u32[]{:S(2)}) collective-permute-start(f32[1024,128]{1,0:T(8,128)S(1)} %broadcast_select_fusion.2), channel_id=1, source_target_pairs={{240,0},{248,8},{0,16},{8,24},{16,32},{24,40},{32,48},{40,56},{48,... | collective-permute-start | bytes 1572872 | tf_op jit(solution)/shard_map/ppermute | solution.py:16
  383.7 15.1 %collective-permute-start.14 = (f32[1024,128]{1,0:T(8,128)S(1)}, f32[1024,128]{1,0:T(8,128)S(1)}, u32[]{:S(2)}, u32[]{:S(2)}) collective-permute-start(f32[1024,128]{1,0:T(8,128)S(1)} %broadcast_select_fusion.11), channel_id=1, source_target_pairs={{32,0},{40,8},{48,16},{56,24},{64,32},{72,40},{80,48},{88,56},{96,... | collective-permute-start | bytes 1572872 | tf_op jit(solution)/shard_map/ppermute | solution.py:16
  396.9 20.9 %collective-permute-start.17 = (f32[1024,128]{1,0:T(8,128)}, f32[1024,128]{1,0:T(8,128)}, u32[]{:S(2)}, u32[]{:S(2)}) collective-permute-start(f32[1024,128]{1,0:T(8,128)} %broadcast_select_fusion.10), channel_id=1, source_target_pairs={{224,0},{232,8},{240,16},{248,24},{0,32},{8,40},{16,48},{24,56},{3... | collective-permute-start | bytes 1572872 | tf_op jit(solution)/shard_map/ppermute | solution.py:16
  414.6 41.4 %copy-start.2 = (f32[128,128]{1,0:T(8,128)S(1)}, f32[128,128]{1,0:T(8,128)}, u32[]{:S(2)}) copy-start(f32[128,128]{1,0:T(8,128)} %reduce-scatter.5.cloned.1.call-done) | copy-start | bytes 196612
  419.8 182.5 %reduce-scatter.11.cloned.1.call-start = ((), (), s32[]{:S(2)}) async-start(), calls=%async_computation.7 | async-start | bytes 589824 | tf_op jit(solution)/shard_map/reduce_scatter | solution.py:67
  488.2 18.6 %collective-permute-start.18 = (f32[1024,128]{1,0:T(8,128)}, f32[1024,128]{1,0:T(8,128)}, u32[]{:S(2)}, u32[]{:S(2)}) collective-permute-start(f32[1024,128]{1,0:T(8,128)} %all_gather.15), channel_id=1, source_target_pairs={{8,0},{16,8},{24,16},{32,24},{40,32},{48,40},{56,48},{64,56},{72,6... | collective-permute-start | bytes 1572872 | tf_op jit(solution)/shard_map/ppermute | solution.py:16
  506.3 11.2 %collective-permute-start.21 = (f32[1024,128]{1,0:T(8,128)S(1)}, f32[1024,128]{1,0:T(8,128)S(1)}, u32[]{:S(2)}, u32[]{:S(2)}) collective-permute-start(f32[1024,128]{1,0:T(8,128)S(1)} %bitcast.101), channel_id=1, source_target_pairs={{248,0},{0,8},{8,16},{16,24},{24,32},{32,40},{40,48},{48,56},{56,6... | collective-permute-start | bytes 1572872 | tf_op jit(solution)/shard_map/ppermute | solution.py:16
  507.9 22.2 %collective-permute-start.19 = (f32[1024,128]{1,0:T(8,128)S(1)}, f32[1024,128]{1,0:T(8,128)S(1)}, u32[]{:S(2)}, u32[]{:S(2)}) collective-permute-start(f32[1024,128]{1,0:T(8,128)S(1)} %broadcast_select_fusion.1), channel_id=1, source_target_pairs={{16,0},{24,8},{32,16},{40,24},{48,32},{56,40},{64,48},{72,56},{80,... | collective-permute-start | bytes 1572872 | tf_op jit(solution)/shard_map/ppermute | solution.py:16
  517.5 25.0 %collective-permute-start.22 = (f32[1024,128]{1,0:T(8,128)S(1)}, f32[1024,128]{1,0:T(8,128)S(1)}, u32[]{:S(2)}, u32[]{:S(2)}) collective-permute-start(f32[1024,128]{1,0:T(8,128)S(1)} %broadcast_select_fusion), channel_id=1, source_target_pairs={{240,0},{248,8},{0,16},{8,24},{16,32},{24,40},{32,48},{40,56},{48,... | collective-permute-start | bytes 1572872 | tf_op jit(solution)/shard_map/ppermute | solution.py:16
  530.2 14.7 %collective-permute-start.20 = (f32[1024,128]{1,0:T(8,128)S(1)}, f32[1024,128]{1,0:T(8,128)S(1)}, u32[]{:S(2)}, u32[]{:S(2)}) collective-permute-start(f32[1024,128]{1,0:T(8,128)S(1)} %broadcast_select_fusion.9), channel_id=1, source_target_pairs={{32,0},{40,8},{48,16},{56,24},{64,32},{72,40},{80,48},{88,56},{96,... | collective-permute-start | bytes 1572872 | tf_op jit(solution)/shard_map/ppermute | solution.py:16
  543.4 20.4 %collective-permute-start.23 = (f32[1024,128]{1,0:T(8,128)}, f32[1024,128]{1,0:T(8,128)}, u32[]{:S(2)}, u32[]{:S(2)}) collective-permute-start(f32[1024,128]{1,0:T(8,128)} %broadcast_select_fusion.8), channel_id=1, source_target_pairs={{224,0},{232,8},{240,16},{248,24},{0,32},{8,40},{16,48},{24,56},{3... | collective-permute-start | bytes 1572872 | tf_op jit(solution)/shard_map/ppermute | solution.py:16
Sparse Core Ops, SparseCore 0:
  123.3 39.8 reduce-scatter.4
  273.2 36.1 reduce-scatter.6
  419.9 36.1 reduce-scatter.8
  566.0 36.2 reduce-scatter.10
where the time goes:
time: 619 us; the launch traced here: 611 us
  waiting for transfers between devices  222 us (36%)
  blocking collectives  125 us (20%)
  matrix products  87.2 us (14%)
  starting transfers between devices  73.7 us (12%)
  local copies, waits for them, and re-layouts  57.9 us (9%)
  other arithmetic  31.1 us (5%)
  between operations  13.7 us (2%)
    reduce_scatter x4, waiting for transfers between devices, fold(): return lax.psum_scatter(terms, 'off', scatter_dimension=0, tiled=True)  149 us
    all_gather x4, blocking collectives, spread(): return lax.all_gather(piece, 'off', axis=0, tiled=True)  125 us
    ppermute x24, starting transfers between devices, passed_along(): return lax.ppermute(block, axis, route)  73.5 us
    ppermute x24, waiting for transfers between devices, passed_along(): return lax.ppermute(block, axis, route)  73.1 us
    dot_general x4, matrix products, apply_tiles(): jnp.einsum('kab,kav->kbv', stored, own[row_list], precision=lax.Precision...  31.5 us
    dot_general x4, matrix products, apply_tiles(): jnp.einsum('kab,kbv->kav', stored, far_field[col_list], precision=lax.Pre...  31.5 us
    dot_general x4, local copies, waits for them, and re-layouts, apply_tiles(): jnp.einsum('kab,kbv->kav', stored, far_field[col_list], precision=lax.Pre...  14.3 us
    dot_general x4, local copies, waits for them, and re-layouts, apply_tiles(): jnp.einsum('kab,kav->kbv', stored, own[row_list], precision=lax.Precision...  14.3 us
  transfers between devices with their start and end apart: 28, of which 12 were waited for; matrix products, arithmetic and copies ran while one was open for 27% of the time, Pallas kernels for 0%

commit v1 on v0

v1 whole, which is shorter than its diff:
```python
import functools

import jax
import jax.numpy as jnp
from jax import lax
from jax.experimental import pallas as pl
from jax.experimental.pallas import tpu as pltpu
from jax.sharding import PartitionSpec as P

DEGREE = 4
MESH = pl.DeviceIdType.MESH

first_scale = 0.4
later_scale = 0.8


def split(x):
    hi = x.astype(jnp.bfloat16)
    lo = (x - hi.astype(jnp.float32)).astype(jnp.bfloat16)
    return hi, lo


def kernel(
    n_row, n_off, bs, chunk,
    where_ref, vec_ref, blocks_hbm, out_ref,
    blocks, a_hi, a_lo, t_hi, t_lo, cur, near, far, xb, ahead, back, got_ahead, got_back,
    load_sem, near_send, far_send, near_recv, far_recv, ahead_send, back_send, ahead_recv, back_recv,
):
    row = lax.axis_index("row")
    off = lax.axis_index("off")
    rows = n_off * bs
    per_chunk = chunk // bs

    def at_row(r):
        return lax.rem(r + n_row, n_row)

    load = pltpu.make_async_copy(blocks_hbm, blocks, load_sem)
    load.start()

    barrier = pltpu.get_barrier_semaphore()
    for s in range(1, n_off):
        pl.semaphore_signal(
            barrier, inc=1, device_id=(row, lax.rem(off + s, n_off)), device_id_type=MESH
        )
        pl.semaphore_signal(barrier, inc=1, device_id=(at_row(row - s), s), device_id_type=MESH)

    @pl.when(off > 0)
    def _():
        for t in range(n_off):
            pl.semaphore_signal(
                barrier, inc=1, device_id=(at_row(row + off), t), device_id_type=MESH
            )

    cur[0] = vec_ref[...]
    cur[1] = jnp.zeros_like(cur[1])

    @pl.when(off > 0)
    def _():
        pl.semaphore_wait(barrier, 3 * n_off - 2)

    @pl.when(off == 0)
    def _():
        pl.semaphore_wait(barrier, 2 * n_off - 2)

    def near_copy(par, s):
        return pltpu.make_async_remote_copy(
            src_ref=cur.at[par],
            dst_ref=near.at[par, off],
            send_sem=near_send.at[s],
            recv_sem=near_recv.at[par, off],
            device_id=(row, lax.rem(off + s, n_off)),
            device_id_type=MESH,
        )

    def far_copy(par, s):
        return pltpu.make_async_remote_copy(
            src_ref=cur.at[par],
            dst_ref=far.at[par, off],
            send_sem=far_send.at[s],
            recv_sem=far_recv.at[par, off],
            device_id=(at_row(row - s), s),
            device_id_type=MESH,
        )

    def send_piece(par):
        for s in range(1, n_off):
            near_copy(par, s).start()
        for s in range(n_off - 1, 0, -1):
            far_copy(par, s).start()

    def await_slot(ref, sem):
        pltpu.make_async_remote_copy(
            src_ref=ref, dst_ref=ref, send_sem=near_send.at[0], recv_sem=sem,
            device_id=(row, lax.rem(off + 1, n_off)), device_id_type=MESH,
        ).wait_recv()

    def back_copy(par, t):
        return pltpu.make_async_remote_copy(
            src_ref=back.at[t],
            dst_ref=got_back.at[par, off],
            send_sem=back_send.at[t],
            recv_sem=back_recv.at[par, off],
            device_id=(at_row(row + off), t),
            device_id_type=MESH,
        )

    def ahead_copy(par, t):
        return pltpu.make_async_remote_copy(
            src_ref=ahead.at[t],
            dst_ref=got_ahead.at[par, off],
            send_sem=ahead_send.at[t],
            recv_sem=ahead_recv.at[par, off],
            device_id=(row, t),
            device_id_type=MESH,
        )

    def wait_back(par):
        @pl.when(off > 0)
        def _():
            for t in range(n_off):
                back_copy(par, t).wait_send()

    def wait_ahead(par):
        for s in range(1, n_off):
            ahead_copy(par, lax.rem(off + s, n_off)).wait_send()

    send_piece(0)
    load.wait()

    def dense_row(r, carry):
        for c in range(n_off):
            k = where_ref[r * n_off + c]
            block = jnp.where(k > 0, blocks[jnp.maximum(k - 1, 0)], 0.0)
            hi, lo = split(block)
            at = pl.ds(pl.multiple_of(r * bs, bs), bs)
            a_hi[at, c * bs:(c + 1) * bs] = hi
            a_lo[at, c * bs:(c + 1) * bs] = lo
            hi, lo = split(block.T)
            t_hi[c * bs:(c + 1) * bs, at] = hi
            t_lo[c * bs:(c + 1) * bs, at] = lo
        return carry

    lax.fori_loop(0, n_off, dense_row, 0)

    def put(t, x):
        hi, lo = split(x)
        at = pl.ds(pl.multiple_of(t * bs, bs), bs)
        xb[at, :bs] = hi
        xb[at, bs:] = lo

    def product(hi_ref, lo_ref, at):
        both = jnp.dot(hi_ref[at, :], xb[...], preferred_element_type=jnp.float32)
        both += jnp.dot(lo_ref[at, :], xb[...], preferred_element_type=jnp.float32)
        return both[:, :bs] + both[:, bs:]

    n_chunks = rows // chunk

    def step(k, carry):
        par = lax.rem(k, 2)
        put(off, cur[par])

        def take_near(s, carry):
            j = lax.rem(off + s, n_off)
            await_slot(near.at[par, j], near_recv.at[par, j])
            put(j, near[par, j])
            return carry

        lax.fori_loop(1, n_off, take_near, 0)

        @pl.when(k > 0)
        def _():
            wait_back(par)

        def back_chunk(c, carry):
            at = pl.ds(pl.multiple_of(c * chunk, chunk), chunk)
            y = product(t_hi, t_lo, at)
            for p in range(per_chunk):
                t = c * per_chunk + p
                back[t] = y[p * bs:(p + 1) * bs]

                @pl.when(off > 0)
                def _():
                    back_copy(par, t).start()
            return carry

        lax.fori_loop(0, n_chunks, back_chunk, 0)

        @pl.when(off > 0)
        def _():
            def take_far(j, carry):
                await_slot(far.at[par, j], far_recv.at[par, j])
                put(j, far[par, j])
                return carry

            lax.fori_loop(0, n_off, take_far, 0)

        @pl.when(k > 0)
        def _():
            wait_ahead(par)

        def ahead_chunk(c, carry):
            at = pl.ds(pl.multiple_of(c * chunk, chunk), chunk)
            y = product(a_hi, a_lo, at)
            for p in range(per_chunk):
                t = c * per_chunk + p
                ahead[t] = y[p * bs:(p + 1) * bs] + jnp.where(off == 0, back[t], 0.0)

                @pl.when(t != off)
                def _():
                    ahead_copy(par, t).start()
            return carry

        lax.fori_loop(0, n_chunks, ahead_chunk, 0)

        total = ahead[off]
        for s in range(1, n_off):
            j = lax.rem(off + s, n_off)
            await_slot(got_ahead.at[par, j], ahead_recv.at[par, j])
            total += got_ahead[par, j]
        for s in range(1, n_off):
            await_slot(got_back.at[par, s], back_recv.at[par, s])
            total += got_back[par, s]
        scale = jnp.where(k == 0, first_scale, later_scale)
        nxt = lax.rem(k + 1, 2)
        cur[nxt] = scale * total - cur[nxt]

        for s in range(1, n_off):
            near_copy(par, s).wait_send()
            far_copy(par, s).wait_send()

        @pl.when(k < DEGREE - 1)
        def _():
            send_piece(nxt)

        return carry

    lax.fori_loop(0, DEGREE, step, 0)
    wait_back(0)
    wait_ahead(0)
    out_ref[...] = cur[DEGREE % 2]


def solution(mesh):
    n_row, n_off = mesh.shape["row"], mesh.shape["off"]

    def per_device(vectors, blocks, lists):
        bs, width = vectors.shape
        rows = n_off * bs
        count = blocks.shape[2]
        position = lists[0, 0, 0] * n_off + lists[0, 0, 1]
        hit = position[None, :] == jnp.arange(n_off * n_off, dtype=jnp.int32)[:, None]
        where = jnp.sum(
            jnp.where(hit, jnp.arange(1, count + 1, dtype=jnp.int32)[None, :], 0),
            axis=1, dtype=jnp.int32,
        )
        f32, bf16 = jnp.float32, jnp.bfloat16
        dma = pltpu.SemaphoreType.DMA
        return pl.pallas_call(
            functools.partial(kernel, n_row, n_off, bs, 2 * bs),
            out_shape=jax.ShapeDtypeStruct((bs, width), f32),
            in_specs=[
                pl.BlockSpec(memory_space=pltpu.SMEM),
                pl.BlockSpec(memory_space=pltpu.VMEM),
                pl.BlockSpec(memory_space=pl.ANY),
            ],
            out_specs=pl.BlockSpec(memory_space=pltpu.VMEM),
            scratch_shapes=[
                pltpu.VMEM((count, bs, bs), f32),
                pltpu.VMEM((rows, rows), bf16),
                pltpu.VMEM((rows, rows), bf16),
                pltpu.VMEM((rows, rows), bf16),
                pltpu.VMEM((rows, rows), bf16),
                pltpu.VMEM((2, bs, width), f32),
                pltpu.VMEM((2, n_off, bs, width), f32),
                pltpu.VMEM((2, n_off, bs, width), f32),
                pltpu.VMEM((rows, 2 * width), bf16),
                pltpu.VMEM((n_off, bs, width), f32),
                pltpu.VMEM((n_off, bs, width), f32),
                pltpu.VMEM((2, n_off, bs, width), f32),
                pltpu.VMEM((2, n_off, bs, width), f32),
                dma,
                dma((n_off,)),
                dma((n_off,)),
                dma((2, n_off)),
                dma((2, n_off)),
                dma((n_off,)),
                dma((n_off,)),
                dma((2, n_off)),
                dma((2, n_off)),
            ],
            compiler_params=pltpu.CompilerParams(collective_id=0, has_side_effects=True),
        )(where, vectors, blocks[0, 0])

    return jax.shard_map(
        per_device,
        mesh=mesh,
        in_specs=(
            P(("row", "off"), None),
            P("row", "off", None, None, None),
            P("row", "off", None, None),
        ),
        out_specs=P(("row", "off"), None),
        check_vma=False,
    )
```

time: 619 us -> 160 us (0.26)
  waiting for transfers between devices: 222 us -> 0 us
  Pallas kernels: 0 us -> 155 us
  blocking collectives: 125 us -> 0 us
  matrix products: 87.2 us -> 0 us
  starting transfers between devices: 73.7 us -> 0 us
  local copies, waits for them, and re-layouts: 57.9 us -> 1.47 us
  other arithmetic: 31.1 us -> 1.37 us
  between operations: 13.7 us -> 0.01 us
    pallas_call x0 -> x1, Pallas kernels: none -> 155 us  [per_device(): pl.pallas_call(functools.partial(kernel, n_row, n_off, bs, 2 * bs), out_s...]
    reduce_scatter x4 -> x0, waiting for transfers between devices: 149 us -> none  [fold(): return lax.psum_scatter(terms, 'off', scatter_dimension=0, tiled=True)]
    all_gather x4 -> x0, blocking collectives: 125 us -> none  [spread(): return lax.all_gather(piece, 'off', axis=0, tiled=True)]
    dot_general x16 -> x0, matrix products: 87.2 us -> none  [the longest x4 31.5 us: apply_tiles(): jnp.einsum('kab,kav->kbv', stored, own[row_list], precision=lax.Precision...]
    ppermute x24 -> x0, starting transfers between devices: 73.5 us -> none  [passed_along(): return lax.ppermute(block, axis, route)]
    ppermute x24 -> x0, waiting for transfers between devices: 73.1 us -> none  [passed_along(): return lax.ppermute(block, axis, route)]
    dot_general x16 -> x0, local copies, waits for them, and re-layouts: 30.2 us -> none  [the longest x4 14.3 us: apply_tiles(): jnp.einsum('kab,kbv->kav', stored, far_field[col_list], precision=lax.Pre...]
    gather x8 -> x0, local copies, waits for them, and re-layouts: 27.7 us -> none  [the longest x4 13.9 us: apply_tiles(): own[row_list]]
  transfers between devices with their start and end apart: 28 -> 0, of which waited for: 12 -> 0; matrix products, arithmetic and copies ran while one was open for 27% -> 0% of each run, Pallas kernels for 0% -> 0%
where the time goes in v1:
time: 160 us; the launch traced here: 158 us
  Pallas kernels  155 us (97%)
    pallas_call x1, Pallas kernels, per_device(): pl.pallas_call(functools.partial(kernel, n_row, n_off, bs, 2 * bs), out_s...  155 us

profile of v1, /device:TPU:32, one launch (start us, length us, event | category | flops | bytes accessed | tf_op | source)
XLA Modules:
  0.0 157.6 jit_solution(4542123025595402499)
XLA Ops:
  0.0 0.8 add_bitcast_fusion
  0.8 0.6 select_reduce_fusion.where_ref
  1.4 154.8 %shard_map.37 = f32[128,128]{1,0:T(8,128)} custom-call(s32[64]{0:T(128)} %select_reduce_fusion.where_ref, f32[128,128]{1,0:T(8,128)} %vec_ref.1, f32[48,128,128]{2,1,0:T(8,128)} %bitcast.3), custom_call_target="tpu_custom_call" | custom-call | tf_op jit(solution)/shard_map/pallas_call | solution.py:258
  156.2 1.5 copy.5
  (1 shorter events, 0.0 us)

commit v2 on v1

v2 whole, which is shorter than its diff:
```python
import functools

import jax
import jax.numpy as jnp
from jax import lax
from jax.experimental import pallas as pl
from jax.experimental.pallas import tpu as pltpu
from jax.sharding import PartitionSpec as P

DEGREE = 4
CHAINS = 2
MESH = pl.DeviceIdType.MESH

first_scale = 0.4
later_scale = 0.8


def split(x):
    hi = x.astype(jnp.bfloat16)
    lo = (x - hi.astype(jnp.float32)).astype(jnp.bfloat16)
    return hi, lo


def swap_halves(x):
    return pltpu.roll(x, x.shape[1] // 2, 1)


def left_of(shape):
    return lax.broadcasted_iota(jnp.int32, shape, 1) < shape[1] // 2


def kernel(
    n_row, n_off, bs, chunk,
    where_ref, vec_ref, blocks_hbm, out_ref,
    blocks, a_hi, a_lo, t_hi, t_lo, cur, near, far, xb, ahead, back, got_ahead, got_back,
    load_sem, near_send, far_send, near_recv, far_recv, ahead_send, back_send, ahead_recv, back_recv,
):
    row = lax.axis_index("row")
    off = lax.axis_index("off")
    rows = n_off * bs
    half = bs // 2
    per_chunk = chunk // bs
    n_chunks = rows // chunk
    left = left_of((half, bs))

    def at_row(r):
        return lax.rem(r + n_row, n_row)

    load = pltpu.make_async_copy(blocks_hbm, blocks, load_sem)
    load.start()

    barrier = pltpu.get_barrier_semaphore()
    for s in range(1, n_off):
        pl.semaphore_signal(
            barrier, inc=1, device_id=(row, lax.rem(off + s, n_off)), device_id_type=MESH
        )
        pl.semaphore_signal(barrier, inc=1, device_id=(at_row(row - s), s), device_id_type=MESH)

    @pl.when(off > 0)
    def _():
        for t in range(n_off):
            pl.semaphore_signal(
                barrier, inc=1, device_id=(at_row(row + off), t), device_id_type=MESH
            )

    upper, lower = vec_ref[:half, :], vec_ref[half:, :]
    cur[0, 0] = jnp.where(left, upper, swap_halves(lower))
    cur[1, 0] = jnp.where(left, swap_halves(upper), lower)
    for h in range(CHAINS):
        cur[h, 1] = jnp.zeros((half, bs), jnp.float32)

    @pl.when(off > 0)
    def _():
        pl.semaphore_wait(barrier, 3 * n_off - 2)

    @pl.when(off == 0)
    def _():
        pl.semaphore_wait(barrier, 2 * n_off - 2)

    def near_copy(h, par, s):
        return pltpu.make_async_remote_copy(
            src_ref=cur.at[h, par],
            dst_ref=near.at[h, par, off],
            send_sem=near_send.at[h, s],
            recv_sem=near_recv.at[h, par, off],
            device_id=(row, lax.rem(off + s, n_off)),
            device_id_type=MESH,
        )

    def far_copy(h, par, s):
        return pltpu.make_async_remote_copy(
            src_ref=cur.at[h, par],
            dst_ref=far.at[h, par, off],
            send_sem=far_send.at[h, s],
            recv_sem=far_recv.at[h, par, off],
            device_id=(at_row(row - s), s),
            device_id_type=MESH,
        )

    def back_copy(h, par, t):
        return pltpu.make_async_remote_copy(
            src_ref=back.at[h, t],
            dst_ref=got_back.at[h, par, off],
            send_sem=back_send.at[h, t],
            recv_sem=back_recv.at[h, par, off],
            device_id=(at_row(row + off), t),
            device_id_type=MESH,
        )

    def ahead_copy(h, par, t):
        return pltpu.make_async_remote_copy(
            src_ref=ahead.at[h, t],
            dst_ref=got_ahead.at[h, par, off],
            send_sem=ahead_send.at[h, t],
            recv_sem=ahead_recv.at[h, par, off],
            device_id=(row, t),
            device_id_type=MESH,
        )

    def await_slot(ref, sem):
        pltpu.make_async_remote_copy(
            src_ref=ref, dst_ref=ref, send_sem=near_send.at[0, 0], recv_sem=sem,
            device_id=(row, lax.rem(off + 1, n_off)), device_id_type=MESH,
        ).wait_recv()

    def send_piece(h, par):
        for s in range(1, n_off):
            near_copy(h, par, s).start()
        for s in range(n_off - 1, 0, -1):
            far_copy(h, par, s).start()

    def wait_back(h, par):
        @pl.when(off > 0)
        def _():
            for t in range(n_off):
                back_copy(h, par, t).wait_send()

    def wait_ahead(h, par):
        for s in range(1, n_off):
            ahead_copy(h, par, lax.rem(off + s, n_off)).wait_send()

    for h in range(CHAINS):
        send_piece(h, 0)
    load.wait()

    def dense_row(r, carry):
        for c in range(n_off):
            k = where_ref[r * n_off + c]
            block = jnp.where(k > 0, blocks[jnp.maximum(k - 1, 0)], 0.0)
            hi, lo = split(block)
            at = pl.ds(pl.multiple_of(r * bs, bs), bs)
            a_hi[at, c * bs:(c + 1) * bs] = hi
            a_lo[at, c * bs:(c + 1) * bs] = lo
            hi, lo = split(block.T)
            t_hi[c * bs:(c + 1) * bs, at] = hi
            t_lo[c * bs:(c + 1) * bs, at] = lo
        return carry

    lax.fori_loop(0, n_off, dense_row, 0)

    def put(t, x):
        hi = x.astype(jnp.bfloat16).astype(jnp.float32)
        lo = x - hi
        start = pl.multiple_of(t * bs, bs)
        xb[pl.ds(start, half), :] = jnp.where(left, hi, swap_halves(lo)).astype(jnp.bfloat16)
        xb[pl.ds(start + half, half), :] = jnp.where(left, swap_halves(hi), lo).astype(jnp.bfloat16)

    def product(hi_ref, lo_ref, at):
        both = jnp.dot(hi_ref[at, :], xb[...], preferred_element_type=jnp.float32)
        both += jnp.dot(lo_ref[at, :], xb[...], preferred_element_type=jnp.float32)
        return both + swap_halves(both)

    def packed(y, p):
        return jnp.where(left, y[p * bs:p * bs + half], y[p * bs + half:(p + 1) * bs])

    def multiply(h, par, k):
        put(off, cur[h, par])

        def take_near(s, carry):
            j = lax.rem(off + s, n_off)
            await_slot(near.at[h, par, j], near_recv.at[h, par, j])
            put(j, near[h, par, j])
            return carry

        lax.fori_loop(1, n_off, take_near, 0)

        @pl.when(k > 0)
        def _():
            wait_back(h, par)

        def back_chunk(c, carry):
            at = pl.ds(pl.multiple_of(c * chunk, chunk), chunk)
            y = product(t_hi, t_lo, at)
            for p in range(per_chunk):
                t = c * per_chunk + p
                back[h, t] = packed(y, p)

                @pl.when(off > 0)
                def _():
                    back_copy(h, par, t).start()
            return carry

        lax.fori_loop(0, n_chunks, back_chunk, 0)

        @pl.when(off > 0)
        def _():
            def take_far(j, carry):
                await_slot(far.at[h, par, j], far_recv.at[h, par, j])
                put(j, far[h, par, j])
                return carry

            lax.fori_loop(0, n_off, take_far, 0)

        @pl.when(k > 0)
        def _():
            wait_ahead(h, par)

        def ahead_chunk(c, carry):
            at = pl.ds(pl.multiple_of(c * chunk, chunk), chunk)
            y = product(a_hi, a_lo, at)
            for p in range(per_chunk):
                t = c * per_chunk + p
                ahead[h, t] = packed(y, p) + jnp.where(off == 0, back[h, t], 0.0)

                @pl.when(t != off)
                def _():
                    ahead_copy(h, par, t).start()
            return carry

        lax.fori_loop(0, n_chunks, ahead_chunk, 0)

    def collect(h, par, k):
        total = ahead[h, off]
        for s in range(1, n_off):
            j = lax.rem(off + s, n_off)
            await_slot(got_ahead.at[h, par, j], ahead_recv.at[h, par, j])
            total += got_ahead[h, par, j]
        for s in range(1, n_off):
            await_slot(got_back.at[h, par, s], back_recv.at[h, par, s])
            total += got_back[h, par, s]
        scale = jnp.where(k == 0, first_scale, later_scale)
        nxt = lax.rem(k + 1, 2)
        cur[h, nxt] = scale * total - cur[h, nxt]
        for s in range(1, n_off):
            near_copy(h, par, s).wait_send()
            far_copy(h, par, s).wait_send()

        @pl.when(k < DEGREE - 1)
        def _():
            send_piece(h, nxt)

    def step(k, carry):
        par = lax.rem(k, 2)

        def each(what):
            def one(h, carry):
                what(h, par, k)
                return carry

            lax.fori_loop(0, CHAINS, one, 0)

        each(multiply)
        each(collect)
        return carry

    lax.fori_loop(0, DEGREE, step, 0)
    last = DEGREE % 2
    for h in range(CHAINS):
        wait_back(h, 1 - last)
        wait_ahead(h, 1 - last)
    out_ref[:half, :] = jnp.where(left, cur[0, last], swap_halves(cur[1, last]))
    out_ref[half:, :] = jnp.where(left, swap_halves(cur[0, last]), cur[1, last])


def solution(mesh):
    n_row, n_off = mesh.shape["row"], mesh.shape["off"]

    def per_device(vectors, blocks, lists):
        bs, width = vectors.shape
        rows = n_off * bs
        half = bs // 2
        count = blocks.shape[2]
        position = lists[0, 0, 0] * n_off + lists[0, 0, 1]
        hit = position[None, :] == jnp.arange(n_off * n_off, dtype=jnp.int32)[:, None]
        where = jnp.sum(
            jnp.where(hit, jnp.arange(1, count + 1, dtype=jnp.int32)[None, :], 0),
            axis=1, dtype=jnp.int32,
        )
        f32, bf16 = jnp.float32, jnp.bfloat16
        dma = pltpu.SemaphoreType.DMA
        slots = pltpu.VMEM((CHAINS, 2, n_off, half, width), f32)
        staged = pltpu.VMEM((CHAINS, n_off, half, width), f32)
        return pl.pallas_call(
            functools.partial(kernel, n_row, n_off, bs, 2 * bs),
            out_shape=jax.ShapeDtypeStruct((bs, width), f32),
            in_specs=[
                pl.BlockSpec(memory_space=pltpu.SMEM),
                pl.BlockSpec(memory_space=pltpu.VMEM),
                pl.BlockSpec(memory_space=pl.ANY),
            ],
            out_specs=pl.BlockSpec(memory_space=pltpu.VMEM),
            scratch_shapes=[
                pltpu.VMEM((count, bs, bs), f32),
                pltpu.VMEM((rows, rows), bf16),
                pltpu.VMEM((rows, rows), bf16),
                pltpu.VMEM((rows, rows), bf16),
                pltpu.VMEM((rows, rows), bf16),
                pltpu.VMEM((CHAINS, 2, half, width), f32),
                slots,
                slots,
                pltpu.VMEM((rows, width), bf16),
                staged,
                staged,
                slots,
                slots,
                dma,
                dma((CHAINS, n_off)),
                dma((CHAINS, n_off)),
                dma((CHAINS, 2, n_off)),
                dma((CHAINS, 2, n_off)),
                dma((CHAINS, n_off)),
                dma((CHAINS, n_off)),
                dma((CHAINS, 2, n_off)),
                dma((CHAINS, 2, n_off)),
            ],
            compiler_params=pltpu.CompilerParams(collective_id=0, has_side_effects=True),
        )(where, vectors, blocks[0, 0])

    return jax.shard_map(
        per_device,
        mesh=mesh,
        in_specs=(
            P(("row", "off"), None),
            P("row", "off", None, None, None),
            P("row", "off", None, None),
        ),
        out_specs=P(("row", "off"), None),
        check_vma=False,
    )
```

time: 160 us -> 137 us (0.86)
  Pallas kernels: 155 us -> 132 us
    pallas_call x1, Pallas kernels: 155 us -> 132 us  [per_device(): pl.pallas_call(functools.partial(kernel, n_row, n_off, bs, 2 * bs), out_s...]
where the time goes in v2:
time: 137 us; the launch traced here: 135 us
  Pallas kernels  132 us (96%)
  local copies, waits for them, and re-layouts  1.47 us (1%)
  other arithmetic  1.37 us (1%)
    pallas_call x1, Pallas kernels, per_device(): pl.pallas_call(functools.partial(kernel, n_row, n_off, bs, 2 * bs), out_s...  132 us

profile of v2, /device:TPU:32, one launch (start us, length us, event | category | flops | bytes accessed | tf_op | source)
XLA Modules:
  0.0 135.0 jit_solution(13286004590124284965)
XLA Ops:
  0.0 0.8 add_bitcast_fusion
  0.8 0.6 select_reduce_fusion.where_ref
  1.4 132.1 %shard_map.37 = f32[128,128]{1,0:T(8,128)} custom-call(s32[64]{0:T(128)} %select_reduce_fusion.where_ref, f32[128,128]{1,0:T(8,128)} %vec_ref.1, f32[48,128,128]{2,1,0:T(8,128)} %bitcast.3), custom_call_target="tpu_custom_call" | custom-call | tf_op jit(solution)/shard_map/pallas_call | solution.py:293
  133.5 1.5 %copy.5 = f32[128,128]{1,0:T(8,128)} copy(f32[128,128]{1,0:T(8,128)} %shard_map.37) | data formatting | bytes 131072
  (1 shorter events, 0.0 us)

commit v3 on v2

--- a/solution.py
+++ b/solution.py
@@ -88,12 +88,13 @@
         )
 
     def far_copy(h, par, s):
+        d = 1 + lax.rem(s + off, n_off - 1)
         return pltpu.make_async_remote_copy(
             src_ref=cur.at[h, par],
             dst_ref=far.at[h, par, off],
             send_sem=far_send.at[h, s],
             recv_sem=far_recv.at[h, par, off],
-            device_id=(at_row(row - s), s),
+            device_id=(at_row(row - d), d),
             device_id_type=MESH,
         )
 
@@ -125,9 +126,9 @@
 
     def send_piece(h, par):
         for s in range(1, n_off):
+            far_copy(h, par, s).start()
+        for s in range(1, n_off):
             near_copy(h, par, s).start()
-        for s in range(n_off - 1, 0, -1):
-            far_copy(h, par, s).start()
 
     def wait_back(h, par):
         @pl.when(off > 0)
@@ -188,7 +189,8 @@
         def _():
             wait_back(h, par)
 
-        def back_chunk(c, carry):
+        def back_chunk(i, carry):
+            c = lax.rem(i + off // 2, n_chunks)
             at = pl.ds(pl.multiple_of(c * chunk, chunk), chunk)
             y = product(t_hi, t_lo, at)
             for p in range(per_chunk):
@@ -215,7 +217,8 @@
         def _():
             wait_ahead(h, par)
 
-        def ahead_chunk(c, carry):
+        def ahead_chunk(i, carry):
+            c = lax.rem(i + off // 2 + 1, n_chunks)
             at = pl.ds(pl.multiple_of(c * chunk, chunk), chunk)
             y = product(a_hi, a_lo, at)
             for p in range(per_chunk):

time: 137 us -> 135 us (0.985)
  the two profiles are of different devices: /device:TPU:32 before, /device:TPU:1 now
where the time goes in v3:
time: 135 us
  Pallas kernels  132 us (98%)
  local copies, waits for them, and re-layouts  1.47 us (1%)
  other arithmetic  1.37 us (1%)
    pallas_call x1, Pallas kernels, per_device(): pl.pallas_call(functools.partial(kernel, n_row, n_off, bs, 2 * bs), out_s...  132 us

profile of v3, /device:TPU:1, one launch (start us, length us, event | category | flops | bytes accessed | tf_op | source)
XLA Modules:
  0.0 134.9 jit_solution(9511776424170550933)
XLA Ops:
  0.0 0.8 add_bitcast_fusion
  0.8 0.6 select_reduce_fusion.where_ref
  1.4 132.0 %shard_map.37 = f32[128,128]{1,0:T(8,128)} custom-call(s32[64]{0:T(128)} %select_reduce_fusion.where_ref, f32[128,128]{1,0:T(8,128)} %vec_ref.1, f32[48,128,128]{2,1,0:T(8,128)} %bitcast.3), custom_call_target="tpu_custom_call" | custom-call | tf_op jit(solution)/shard_map/pallas_call | solution.py:296
  133.4 1.5 %copy.5 = f32[128,128]{1,0:T(8,128)} copy(f32[128,128]{1,0:T(8,128)} %shard_map.37) | data formatting | bytes 131072
  (1 shorter events, 0.0 us)

commit v4 on v3

--- a/solution.py
+++ b/solution.py
@@ -126,9 +126,9 @@
 
     def send_piece(h, par):
         for s in range(1, n_off):
+            near_copy(h, par, s).start()
+        for s in range(1, n_off):
             far_copy(h, par, s).start()
-        for s in range(1, n_off):
-            near_copy(h, par, s).start()
 
     def wait_back(h, par):
         @pl.when(off > 0)

time: 135 us -> 134 us (level)
  the two profiles are of different devices: /device:TPU:1 before, /device:TPU:8 now
where the time goes in v4:
time: 134 us
  Pallas kernels  131 us (98%)
  local copies, waits for them, and re-layouts  1.47 us (1%)
  other arithmetic  1.37 us (1%)
    pallas_call x1, Pallas kernels, per_device(): pl.pallas_call(functools.partial(kernel, n_row, n_off, bs, 2 * bs), out_s...  131 us

profile of v4, /device:TPU:8, one launch (start us, length us, event | category | flops | bytes accessed | tf_op | source)
XLA Modules:
  0.0 133.5 jit_solution(3483872285462840040)
XLA Ops:
  0.0 0.8 add_bitcast_fusion
  0.8 0.6 select_reduce_fusion.where_ref
  1.4 130.7 %shard_map.37 = f32[128,128]{1,0:T(8,128)} custom-call(s32[64]{0:T(128)} %select_reduce_fusion.where_ref, f32[128,128]{1,0:T(8,128)} %vec_ref.1, f32[48,128,128]{2,1,0:T(8,128)} %bitcast.3), custom_call_target="tpu_custom_call" | custom-call | tf_op jit(solution)/shard_map/pallas_call | solution.py:296
  132.1 1.5 %copy.5 = f32[128,128]{1,0:T(8,128)} copy(f32[128,128]{1,0:T(8,128)} %shard_map.37) | data formatting | bytes 131072
  (1 shorter events, 0.0 us)
